TPU v7x, 32 devices: a whole 2x2x4 slice. The times are simulated.
32 devices in a mesh: grp: 2 (over x), row: 8 (over z, y), col: 2 (over core).
Axes of the slice: x: 2, y: 2, z: 4, core: 2. Of those that a mesh axis runs over, the one named last changes fastest.
Arguments:
- queries: bfloat16 [8192, 2048], P(('grp', 'row'), 'col'), parts along dimension 0, may hold values from -34 to 34
- keys: bfloat16 [8192, 1024], P(('grp', 'row'), 'col'), parts along dimension 0, may hold values from -34 to 34
- values: bfloat16 [8192, 1024], P(('grp', 'row'), 'col'), parts along dimension 0, may hold values from -6 to 6
- out_proj: bfloat16 [2048, 5376], P(('col', 'row'))
- post_gain: float32 [5376], P('col'), may hold values from 0.1 to 1.9
- mean_vec: float32 [5376], P('col'), may hold values from -5 to 5
- erase_in: float32 [5376, 64], P('col'), may hold values from -0.078125 to 0.078125
- erase_out: float32 [5376, 64], P('col'), may hold values from -0.375 to 0.375
Outputs:
- erased: bfloat16 [8192, 5376], P(('grp', 'row'), 'col'), parts along dimension 0
There are 2 independent parts, one for each index of `grp`. A program takes and returns all parts, laid end to end along the dimension named above; an argument that names none is the same for every part. Nothing has to cross between parts.
All inputs are finite; a program needn't handle non-finite values.
Results may differ from a plain program's by a relative error of at most 0.012.
The roundings to bfloat16 on the way count: a program that leaves them out, or rounds other values in their place, can miss the bound.
Values may be sent and summed in bfloat16 or wider, within the bound.
A program may use at most 128 MiB of HBM per device.

v0:
```python
import jax
import jax.numpy as jnp
from jax import lax
from jax.sharding import PartitionSpec as P

D = 5376
HD = 128
WINDOW = 1024


query_scale = 168.0 ** (-0.5)
norm_eps = 1e-06
rope_base = 10000.0


def shifted(block, axis, distance):
    devices = range(lax.axis_size(axis))
    route = [(i - distance, i) for i in devices if i - distance in devices]
    return lax.ppermute(block, axis, route)


def rotate(field, positions):
    half_dim = HD // 2
    inverse = jnp.exp(
        -(2.0 * jnp.arange(half_dim, dtype=jnp.float32) / HD) * jnp.log(jnp.float32(rope_base))
    )
    angles = positions[:, None] * inverse[None, :]
    cosine = jnp.cos(angles)[:, None, :]
    sine = jnp.sin(angles)[:, None, :]
    wide = field.astype(jnp.float32)
    first = wide[..., :half_dim]
    second = wide[..., half_dim:]
    return jnp.concatenate(
        [first * cosine - second * sine, second * cosine + first * sine], -1
    ).astype(jnp.bfloat16)


def on_device(queries, keys, values, out_proj, post_gain, mean_vec, erase_in, erase_out):
    tok_rows = queries.shape[0]
    head_local = queries.shape[1] // HD
    kv_local = keys.shape[1] // HD
    group = head_local // kv_local
    first_row = lax.axis_index("row") * tok_rows
    positions = (first_row + jnp.arange(tok_rows, dtype=jnp.int32)).astype(jnp.float32)
    q_rot = rotate(queries.reshape(tok_rows, head_local, HD), positions)
    k_rot = rotate(keys.reshape(tok_rows, kv_local, HD), positions).reshape(tok_rows, kv_local * HD)
    hop_count = WINDOW // tok_rows
    received = []
    for hop_index in range(1, hop_count + 1):
        received.append(shifted((k_rot, values), "row", hop_index))
    key_all = jnp.concatenate([pair[0] for pair in reversed(received)] + [k_rot], 0)
    val_all = jnp.concatenate([pair[1] for pair in reversed(received)] + [values], 0)
    key_count = key_all.shape[0]
    key_pos = first_row - hop_count * tok_rows + jnp.arange(key_count, dtype=jnp.int32)
    query_pos = first_row + jnp.arange(tok_rows, dtype=jnp.int32)
    offsets = query_pos[:, None] - key_pos[None, :]
    allowed = ((key_pos >= 0)[None, :] & (offsets >= 0) & (offsets < WINDOW))[None]
    outputs = []
    for kv_slot in range(kv_local):
        query_group = q_rot[:, kv_slot * group : (kv_slot + 1) * group, :]
        key_group = key_all[:, kv_slot * HD : (kv_slot + 1) * HD]
        val_group = val_all[:, kv_slot * HD : (kv_slot + 1) * HD]
        scores = (
            jnp.einsum("tgd,sd->gts", query_group, key_group, preferred_element_type=jnp.float32)
            * query_scale
        )
        scores = jnp.where(allowed, scores, -1e30)
        row_max = jnp.max(scores, axis=-1, keepdims=True)
        weights = jnp.where(allowed, jnp.exp(scores - row_max), 0.0)
        probs = (weights / jnp.sum(weights, axis=-1, keepdims=True)).astype(jnp.bfloat16)
        mixed = jnp.einsum("gts,sd->tgd", probs, val_group, preferred_element_type=jnp.float32)
        outputs.append(mixed.reshape(tok_rows, group * HD))
    attended = jnp.concatenate(outputs, 1).astype(jnp.bfloat16)
    partial_sum = jnp.dot(
        attended,
        lax.all_gather(out_proj, "row", axis=0, tiled=True),
        preferred_element_type=jnp.float32,
    )
    hidden = lax.psum_scatter(partial_sum, "col", scatter_dimension=1, tiled=True)
    gained = jnp.dot(hidden * post_gain[None, :], erase_in, precision=lax.Precision.HIGHEST)
    mean_code = jnp.dot(mean_vec[None, :], erase_in, precision=lax.Precision.HIGHEST)
    total_sq, gained_sum, mean_sum = lax.psum(
        (jnp.sum(hidden * hidden, axis=1), gained, mean_code), "col"
    )
    inv_rms = lax.rsqrt(total_sq / D + norm_eps)
    normed = hidden * inv_rms[:, None] * post_gain[None, :]
    erase_code = inv_rms[:, None] * gained_sum - mean_sum
    return (normed - jnp.dot(erase_code, erase_out.T, precision=lax.Precision.HIGHEST)).astype(
        jnp.bfloat16
    )


def solution(mesh):
    placed = (
        P(("grp", "row"), "col"),
        P(("grp", "row"), "col"),
        P(("grp", "row"), "col"),
        P(("col", "row"), None),
        P("col"),
        P("col"),
        P("col", None),
        P("col", None),
    )
    return jax.shard_map(
        on_device, mesh=mesh, in_specs=placed, out_specs=P(("grp", "row"), "col"), check_vma=False
    )
```

profile of v0, /device:TPU:5, one launch (start us, length us, event | category | flops | bytes accessed | tf_op | source)
XLA Modules:
  0.0 277.4 jit_solution(11931267085919414568)
XLA Ops:
  12.2 4.0 %collective-permute-start.2 = (bf16[512,512]{1,0:T(8,128)(2,1)}, bf16[512,512]{1,0:T(8,128)(2,1)}, u32[]{:S(2)}, u32[]{:S(2)}) collective-permute-start(bf16[512,512]{1,0:T(8,128)(2,1)} %bitcast.102), channel_id=1, source_target_pairs={{0,4},{2,6},{4,8},{6,10},{8,12},{10,14},{1,5},{3,7},{5,9},{7,11},{... | collective-permute-start | bytes 1572872 | tf_op jit(solution)/shard_map/ppermute | solution.py:19
  16.2 2.3 collective-permute-start.3
  19.6 4.0 %collective-permute-start = (bf16[512,512]{0,1:T(8,128)(2,1)}, bf16[512,512]{0,1:T(8,128)(2,1)}, u32[]{:S(2)}, u32[]{:S(2)}) collective-permute-start(bf16[512,512]{0,1:T(8,128)(2,1)} %copy.16), channel_id=1, source_target_pairs={{0,4},{2,6},{4,8},{6,10},{8,12},{10,14},{1,5},{3,7},{5,9},{7,11},{... | collective-permute-start | bytes 1572872 | tf_op jit(solution)/shard_map/ppermute | solution.py:19
  23.6 2.4 collective-permute-start.1
  26.6 2.0 fusion.19
  30.2 1.8 copy.30
  32.0 3.2 %copy.31 = f32[512,8,64]{2,0,1:T(8,128)} copy(f32[512,8,64]{0,2,1:T(8,128)} %get-tuple-element.11) | data formatting | bytes 2097152
  35.2 3.5 %subtract_convert_fusion.1 = (bf16[512,8,64]{2,0,1:T(8,128)(2,1)}, bf16[512,8,64]{2,0,1:T(8,128)(2,1)}) fusion(f32[512,8,64]{2,0,1:T(8,128)} %copy.31, f32[512,8,64]{2,0,1:T(8,128)S(1)} %copy.30, f32[512,64]{1,0:T(8,128)} %copy-done.3, f32[512,64]{1,0:T(8,128)} %copy-done.2), kind=kLoop, calls=%fused_computation.46 | loop fusion | flops 2097152 | bytes 3407872 | tf_op jit(solution)/shard_map/convert.14
  39.9 14.0 %collective-permute-done.3 = bf16[512,512]{1,0:T(8,128)(2,1)} collective-permute-done((bf16[512,512]{1,0:T(8,128)(2,1)}, bf16[512,512]{1,0:T(8,128)(2,1)}, u32[]{:S(2)}, u32[]{:S(2)}) %collective-permute-start.3) | collective-permute-done | bytes 524320 | tf_op jit(solution)/shard_map/ppermute | solution.py:19
  55.0 21.3 %collective-permute-done = bf16[512,512]{0,1:T(8,128)(2,1)} collective-permute-done((bf16[512,512]{0,1:T(8,128)(2,1)}, bf16[512,512]{0,1:T(8,128)(2,1)}, u32[]{:S(2)}, u32[]{:S(2)}) %collective-permute-start) | collective-permute-done | bytes 524320 | tf_op jit(solution)/shard_map/ppermute | solution.py:19
  76.3 22.5 %collective-permute-done.1 = bf16[512,512]{0,1:T(8,128)(2,1)} collective-permute-done((bf16[512,512]{0,1:T(8,128)(2,1)}, bf16[512,512]{0,1:T(8,128)(2,1)}, u32[]{:S(2)}, u32[]{:S(2)}) %collective-permute-start.1) | collective-permute-done | bytes 524320 | tf_op jit(solution)/shard_map/ppermute | solution.py:19
  100.3 7.4 %fusion.80 = (f32[2,512]{1,0:T(2,128)S(1)}, f32[2,512,1536]{1,2,0:T(8,128)}) fusion(pred[512,1536]{0,1:T(8,128)(4,1)} %fusion.19, bf16[1536,512]{1,0:T(8,128)(2,1)} %copy-done.7, bf16[512,8,64]{2,0,1:T(8,128)(2,1)} %get-tuple-element.8, bf16[512,8,64]{2,0,1:T(8,128)(2,1)S(1)} %copy-done.5), kind=kOutput, calls=%fused_computation.116 | convolution fusion | flops 411043328 | bytes 9834496 | tf_op jit(solution)/shard_map/sub | solution.py:69
  107.7 7.4 %fusion.87 = (f32[2,512]{1,0:T(2,128)S(1)}, f32[2,512,1536]{1,2,0:T(8,128)}) fusion(pred[512,1536]{0,1:T(8,128)(4,1)} %fusion.19, bf16[1536,512]{1,0:T(8,128)(2,1)} %copy-done.7, bf16[512,8,64]{2,0,1:T(8,128)(2,1)S(1)} %copy-done.5, bf16[512,8,64]{2,0,1:T(8,128)(2,1)} %get-tuple-element.8), kind=kOutput, calls=%fused_computation.119 | convolution fusion | flops 411043328 | bytes 9834496 | tf_op jit(solution)/shard_map/sub | solution.py:69
  115.1 7.4 %fusion.84 = (f32[2,512]{1,0:T(2,128)S(1)}, f32[2,512,1536]{1,2,0:T(8,128)}) fusion(pred[512,1536]{0,1:T(8,128)(4,1)} %fusion.19, bf16[1536,512]{1,0:T(8,128)(2,1)} %copy-done.7, bf16[512,8,64]{2,0,1:T(8,128)(2,1)S(1)} %copy-done.5, bf16[512,8,64]{2,0,1:T(8,128)(2,1)} %get-tuple-element.8), kind=kOutput, calls=%fused_computation.118 | convolution fusion | flops 411043328 | bytes 9834496 | tf_op jit(solution)/shard_map/sub | solution.py:69
  122.5 7.7 %fusion.81 = (f32[2,512]{1,0:T(2,128)S(1)}, f32[2,512,1536]{1,2,0:T(8,128)}) fusion(pred[512,1536]{0,1:T(8,128)(4,1)} %fusion.19, bf16[1536,512]{1,0:T(8,128)(2,1)} %copy-done.7, bf16[512,8,64]{2,0,1:T(8,128)(2,1)S(1)} %copy-done.5, bf16[512,8,64]{2,0,1:T(8,128)(2,1)} %get-tuple-element.8), kind=kOutput, calls=%fused_computation.117 | convolution fusion | flops 411043328 | bytes 9834496 | tf_op jit(solution)/shard_map/sub | solution.py:69
  130.1 3.5 %fusion.32 = bf16[128,2,512]{2,0,1:T(8,128)(2,1)S(1)} fusion(f32[2,512,1536]{1,2,0:T(8,128)} %get-tuple-element.22, f32[2,512]{1,0:T(2,128)S(1)} %get-tuple-element.21, bf16[1536,512]{0,1:T(8,128)(2,1)S(1)} %pad_maximum_fusion), kind=kOutput, calls=%fused_computation.51 | convolution fusion | flops 405929984 | bytes 6950912 | tf_op jit(solution)/shard_map/gts,sd->tgd/dot_general | solution.py:71
  139.3 64.3 %all-gather.2.cloned.1.call-done = bf16[1024,5376]{1,0:T(8,128)(2,1)} async-done(((bf16[128,5376]{1,0:T(8,128)(2,1)}), bf16[1024,5376]{1,0:T(8,128)(2,1)}) %all-gather.2.cloned.1.call-update) | async-done | bytes 11010064 | tf_op jit(solution)/shard_map/all_gather | solution.py:76
  203.6 12.6 %fusion.41 = f32[512,5376]{1,0:T(8,128)} fusion(bf16[1024,5376]{1,0:T(8,128)(2,1)} %all-gather.2.cloned.1.call-done, bf16[512,256]{0,1:T(8,128)(2,1)S(1)} %bitcast.109, bf16[512,256]{0,1:T(8,128)(2,1)S(1)} %bitcast.108, bf16[512,256]{0,1:T(8,128)(2,1)S(1)} %bitcast.107, bf16[512,256]{0,1:T(8,128)(2,1)S(1)} %bitcast.106), kind=kOutput, calls=%fused_computation.57 | convolution fusion | flops 5641338880 | bytes 23068672 | tf_op jit(solution)/shard_map/dot_general | solution.py:74
  218.1 17.2 %reduce-scatter.2.cloned.1.call-done = f32[512,2688]{1,0:T(8,128)} async-done(((f32[512,5376]{1,0:T(8,128)}), f32[512,2688]{1,0:T(8,128)}) %reduce-scatter.2.cloned.1.call-update) | async-done | bytes 5505040 | tf_op jit(solution)/shard_map/reduce_scatter | solution.py:79
  235.3 7.8 %fusion.4 = f32[512,64]{1,0:T(8,128)} fusion(f32[2688,64]{0,1:T(8,128)S(1)} %copy-done.1, f32[512,2688]{1,0:T(8,128)} %reduce-scatter.2.cloned.1.call-done, f32[2688]{0:T(1024)S(1)} %copy-done.8), kind=kOutput, calls=%fused_computation.17 | convolution fusion | flops 1058340864 | bytes 6334976 | tf_op jit(solution)/shard_map/dot_general | solution.py:80
  243.1 3.0 %multiply_reduce_fusion = f32[512]{0:T(512)S(1)} fusion(f32[512,2688]{1,0:T(8,128)} %reduce-scatter.2.cloned.1.call-done), kind=kLoop, calls=%fused_computation.19 | loop fusion | flops 2752000 | bytes 5507072 | tf_op jit(solution)/shard_map/reduce_sum | solution.py:83
  246.1 2.5 all-reduce
  248.6 14.2 %all-reduce.3.cloned.1.call-done = f32[512,64]{1,0:T(8,128)} async-done(((f32[512,64]{1,0:T(8,128)}), f32[512,64]{1,0:T(8,128)}) %all-reduce.3.cloned.1.call-update) | async-done | bytes 131088 | tf_op jit(solution)/shard_map/psum | solution.py:82
  262.8 8.0 %subtract_convert_fusion = bf16[512,2688]{1,0:T(8,128)(2,1)} fusion(f32[512,2688]{1,0:T(8,128)} %reduce-scatter.2.cloned.1.call-done, f32[2688,64]{0,1:T(8,128)S(1)} %copy-done, f32[2688]{0:T(1024)S(1)} %copy-done.8, f32[512]{0:T(512)S(1)} %add_rsqrt_fusion, f32[512,64]{1,0:T(8,128)} %all-reduce.3.cloned.1.call-done, f32[64]{0:T(128)S(1)} %get-tuple-element.6), kind=kOutput, calls=%fused_computation.16 | convolution fusion | flops 1062535168 | bytes 9089792 | tf_op jit(solution)/shard_map/dot_general | solution.py:88
  (62 shorter events, 19.9 us)
Async XLA Ops:
  6.5 256.3 %copy-start = (f32[2688,64]{0,1:T(8,128)S(1)}, f32[2688,64]{0,1:T(8,128)}, u32[]{:S(2)}) copy-start(f32[2688,64]{0,1:T(8,128)} %param.15) | copy-start | bytes 2064388
  6.5 12.0 %copy-start.6 = (bf16[512,512]{1,0:T(8,128)(2,1)S(1)}, bf16[512,512]{1,0:T(8,128)(2,1)}, u32[]{:S(2)}) copy-start(bf16[512,512]{1,0:T(8,128)(2,1)} %param.10) | copy-start | bytes 1572868
  6.5 19.4 %copy-start.4 = (bf16[512,1024]{1,0:T(8,128)(2,1)S(1)}, bf16[512,1024]{1,0:T(8,128)(2,1)}, u32[]{:S(2)}) copy-start(bf16[512,1024]{1,0:T(8,128)(2,1)} %param.8) | copy-start | bytes 3145732
  6.5 197.1 %all-gather.2.cloned.1.call-start = ((), (), s32[]{:S(2)}) async-start(), calls=%async_computation.1 | async-start | bytes 12386304 | tf_op jit(solution)/shard_map/all_gather | solution.py:76
  7.3 228.0 %reduce-scatter.2.cloned.1.call-start = ((), (), s32[]{:S(2)}) async-start(), calls=%async_computation.2 | async-start | bytes 16515072 | tf_op jit(solution)/shard_map/reduce_scatter | solution.py:79
  9.7 0.9 copy-start.2
  9.7 0.9 copy-start.3
  12.2 26.5 %collective-permute-start.2 = (bf16[512,512]{1,0:T(8,128)(2,1)}, bf16[512,512]{1,0:T(8,128)(2,1)}, u32[]{:S(2)}, u32[]{:S(2)}) collective-permute-start(bf16[512,512]{1,0:T(8,128)(2,1)} %bitcast.102), channel_id=1, source_target_pairs={{0,4},{2,6},{4,8},{6,10},{8,12},{10,14},{1,5},{3,7},{5,9},{7,11},{... | collective-permute-start | bytes 1572872 | tf_op jit(solution)/shard_map/ppermute | solution.py:19
  16.2 37.7 %collective-permute-start.3 = (bf16[512,512]{1,0:T(8,128)(2,1)}, bf16[512,512]{1,0:T(8,128)(2,1)}, u32[]{:S(2)}, u32[]{:S(2)}) collective-permute-start(bf16[512,512]{1,0:T(8,128)(2,1)} %bitcast.102), channel_id=1, source_target_pairs={{0,2},{2,4},{4,6},{6,8},{8,10},{10,12},{12,14},{1,3},{3,5},{5,7},{... | collective-permute-start | bytes 1572872 | tf_op jit(solution)/shard_map/ppermute | solution.py:19
  19.6 56.7 %collective-permute-start = (bf16[512,512]{0,1:T(8,128)(2,1)}, bf16[512,512]{0,1:T(8,128)(2,1)}, u32[]{:S(2)}, u32[]{:S(2)}) collective-permute-start(bf16[512,512]{0,1:T(8,128)(2,1)} %copy.16), channel_id=1, source_target_pairs={{0,4},{2,6},{4,8},{6,10},{8,12},{10,14},{1,5},{3,7},{5,9},{7,11},{... | collective-permute-start | bytes 1572872 | tf_op jit(solution)/shard_map/ppermute | solution.py:19
  23.6 75.2 %collective-permute-start.1 = (bf16[512,512]{0,1:T(8,128)(2,1)}, bf16[512,512]{0,1:T(8,128)(2,1)}, u32[]{:S(2)}, u32[]{:S(2)}) collective-permute-start(bf16[512,512]{0,1:T(8,128)(2,1)} %copy.16), channel_id=1, source_target_pairs={{0,2},{2,4},{4,6},{6,8},{8,10},{10,12},{12,14},{1,3},{3,5},{5,7},{... | collective-permute-start | bytes 1572872 | tf_op jit(solution)/shard_map/ppermute | solution.py:19
  38.7 61.6 %copy-start.5 = (bf16[512,8,64]{2,0,1:T(8,128)(2,1)S(1)}, bf16[512,8,64]{2,0,1:T(8,128)(2,1)}, u32[]{:S(2)}) copy-start(bf16[512,8,64]{2,0,1:T(8,128)(2,1)} %get-tuple-element.7) | copy-start | bytes 1572868
  55.0 21.3 %copy-start.7 = (bf16[1536,512]{1,0:T(8,128)(2,1)}, bf16[1536,512]{1,0:T(8,128)(2,1)S(1)}, u32[]{:S(2)}) copy-start(bf16[1536,512]{1,0:T(8,128)(2,1)S(1)} %constant_dynamic-update-slice_fusion) | copy-start | bytes 4718596
  130.1 4.6 %copy-start.10 = (f32[2,512,1536]{1,2,0:T(8,128)S(1)}, f32[2,512,1536]{1,2,0:T(8,128)}, u32[]{:S(2)}) copy-start(f32[2,512,1536]{1,2,0:T(8,128)} %get-tuple-element.20) | copy-start | bytes 18874372
  130.1 5.8 %slice-start.2 = ((s8[6291456]{0:T(1024)(128)(4,1)}), s8[4194304]{0:T(1024)(128)(4,1)S(1)}, s32[]{:S(2)}) async-start(s8[6291456]{0:T(1024)(128)(4,1)} %bitcast.112), calls=%async_computation.6 | async-start | bytes 8388608
  134.8 2.1 slice-start.3
  134.8 3.3 %slice-start = ((s8[6291456]{0:T(1024)(128)(4,1)}), s8[4194304]{0:T(1024)(128)(4,1)S(1)}, s32[]{:S(2)}) async-start(s8[6291456]{0:T(1024)(128)(4,1)} %bitcast.110), calls=%async_computation.4 | async-start | bytes 8388608
  136.9 1.8 slice-start.1
  216.3 0.7 copy-start.9
  216.3 1.1 copy-start.1
  216.3 19.0 %copy-start.8 = (f32[2688]{0:T(1024)S(1)}, f32[2688]{0:T(1024)}, u32[]{:S(2)}) copy-start(f32[2688]{0:T(1024)} %param.12) | copy-start | bytes 32260
  216.3 46.5 %all-reduce.3.cloned.1.call-start = ((), (), s32[]{:S(2)}) async-start(), calls=%async_computation.3 | async-start | bytes 524288 | tf_op jit(solution)/shard_map/psum | solution.py:82
Sparse Core Ops, SparseCore 0:
  9.5 194.0 all-gather.1
  216.4 18.8 reduce-scatter.1
  243.2 19.5 all-reduce.2
where the time goes:
time: 279 us; the launch traced here: 277 us
  waiting for transfers between devices  154 us (55%)
  matrix products  64.3 us (23%)
  local copies, waits for them, and re-layouts  17.3 us (6%)
  between operations  13.3 us (5%)
  starting transfers between devices  13 us (5%)
  other arithmetic  12.6 us (5%)
    all_gather x1, waiting for transfers between devices, on_device(): lax.all_gather(out_proj, 'row', axis=0, tiled=True)  64.3 us
    ppermute x4, waiting for transfers between devices, shifted(): return lax.ppermute(block, axis, route)  57.8 us
    sub x4, matrix products, on_device(): weights = jnp.where(allowed, jnp.exp(scores - row_max), 0.0)  29.9 us
    reduce_scatter x1, waiting for transfers between devices, on_device(): lax.psum_scatter(partial_sum, 'col', scatter_dimension=1, tiled=True)  17.2 us
    unnamed x38, local copies, waits for them, and re-layouts  14.3 us
    psum x1, waiting for transfers between devices, on_device(): lax.psum((jnp.sum(hidden * hidden, axis=1), gained, mean_code), 'col')  14.2 us
    ppermute x4, starting transfers between devices, shifted(): return lax.ppermute(block, axis, route)  12.7 us
    dot_general x1, matrix products, on_device(): jnp.dot(attended, lax.all_gather(out_proj, 'row', axis=0, tiled=True), pr...  12.6 us
  transfers between devices with their start and end apart: 7, of which 6 were waited for; matrix products, arithmetic and copies ran while one was open for 22% of the time, Pallas kernels for 0%

commit v1 on v0

v1 whole, which is shorter than its diff:
```python
import functools

import jax
import jax.numpy as jnp
import numpy as np
from jax import lax
from jax.experimental import pallas as pl
from jax.experimental.pallas import tpu as pltpu
from jax.sharding import PartitionSpec as P

HD = 128
WINDOW = 1024
MESH = pl.DeviceIdType.MESH
query_scale = 168.0 ** (-0.5)
norm_eps = 1e-06
rope_base = 10000.0
QB = 256
TN = 384
BIG = 1e30


def split_cat(x):
    hi = x.astype(jnp.bfloat16).astype(jnp.float32)
    return jnp.concatenate([hi, x - hi], axis=1).astype(jnp.bfloat16)


def hi_lo(x):
    hi = x.astype(jnp.bfloat16)
    return hi, (x - hi.astype(jnp.float32)).astype(jnp.bfloat16)


def kernel(n_row, d_full, q_hbm, k_hbm, v_hbm, w_hbm, gain_ref, mean_ref, ein_ref, eout_ref, inv_ref,
           out_ref, qbuf, kbuf, vbuf, krot, wbuf, att, hidden, cosb, sinb, ein_cat, eout_cat,
           st_send, st_recv, loc_sem, wr_sem, ws_sem, kr_sem, ks_sem, as_sem, ar_sem, ss_sem, sr_sem):
    nz = n_row // 2
    g, r, f = lax.axis_index("grp"), lax.axis_index("row"), lax.axis_index("col")
    zz, yy = r // 2, r % 2
    has_up, has_dn = zz < nz - 1, zz > 0
    tok = qbuf.shape[0]
    rows, half = wbuf.shape[1], wbuf.shape[2]
    heads = qbuf.shape[1] // HD
    kvh = kbuf.shape[2] // HD
    acols = heads * HD
    n_tile = half // TN

    part = {"grp": g, "row": r, "col": 1 - f}
    xnb = {"grp": 1 - g, "row": r, "col": f}
    ynb = {"grp": g, "row": 2 * zz + 1 - yy, "col": f}
    up = {"grp": g, "row": r + 2, "col": f}
    dn = {"grp": g, "row": r - 2, "col": f}

    barrier = pltpu.get_barrier_semaphore()
    for nb in (part, xnb, ynb):
        pl.semaphore_signal(barrier, inc=1, device_id=nb, device_id_type=MESH)

    @pl.when(has_up)
    def _():
        pl.semaphore_signal(barrier, inc=1, device_id=up, device_id_type=MESH)

    @pl.when(has_dn)
    def _():
        pl.semaphore_signal(barrier, inc=1, device_id=dn, device_id_type=MESH)

    u_own = f * n_row + r
    loc = [
        pltpu.make_async_copy(w_hbm.at[:, pl.ds(pl.multiple_of(f * half, 128), half)], wbuf.at[u_own], loc_sem.at[0]),
        pltpu.make_async_copy(k_hbm, kbuf.at[2], loc_sem.at[1]),
        pltpu.make_async_copy(q_hbm, qbuf, loc_sem.at[2]),
        pltpu.make_async_copy(v_hbm, vbuf.at[2], loc_sem.at[3]),
    ]
    for c in loc:
        c.start()

    pl.semaphore_wait(barrier, 3 + has_up.astype(jnp.int32) + has_dn.astype(jnp.int32))

    pending = []

    def send(cond, make):
        pending.append((cond, make))
        if cond is None:
            make().start()
        else:
            @pl.when(cond)
            def _():
                make().start()

    n_ws = [0]

    def send_w(cond, u, dev, src=None):
        i = n_ws[0]
        n_ws[0] += 1

        def make():
            return pltpu.make_async_remote_copy(
                src_ref=wbuf.at[u] if src is None else src(), dst_ref=wbuf.at[u],
                send_sem=ws_sem.at[i], recv_sem=wr_sem.at[u], device_id=dev, device_id_type=MESH)

        send(cond, make)

    n_ks = [0]

    def send_kv(cond, src, buf, slot, which, dev):
        i = n_ks[0]
        n_ks[0] += 1

        def make():
            return pltpu.make_async_remote_copy(
                src_ref=src(), dst_ref=buf.at[slot], send_sem=ks_sem.at[i],
                recv_sem=kr_sem.at[2 * slot + which], device_id=dev, device_id_type=MESH)

        send(cond, make)

    def wait_w(u):
        pltpu.make_async_copy(wbuf.at[u], wbuf.at[u], wr_sem.at[u]).wait()

    def wait_kv(slot):
        pltpu.make_async_copy(kbuf.at[slot], kbuf.at[slot], kr_sem.at[2 * slot]).wait()
        pltpu.make_async_copy(vbuf.at[slot], vbuf.at[slot], kr_sem.at[2 * slot + 1]).wait()

    send_w(None, u_own, part, lambda: w_hbm.at[:, pl.ds(pl.multiple_of((1 - f) * half, 128), half)])
    send_kv(yy == 0, lambda: k_hbm, kbuf, 1, 0, ynb)
    send_kv(yy == 0, lambda: v_hbm, vbuf, 1, 1, ynb)
    send_kv(has_up, lambda: k_hbm, kbuf, 0, 0, up)

    def unit(c, z, y):
        return c * n_row + 2 * z + y

    u_line = unit(g, zz, yy)
    u_other = unit(1 - g, zz, yy)
    loc[0].wait()
    wait_w(unit(1 - f, zz, yy))
    send_w(has_up, u_line, up)
    send_w(has_dn, u_line, dn)
    send_kv(has_up, lambda: v_hbm, vbuf, 0, 1, up)
    send_w(None, u_line, ynb)

    @pl.when(zz == 0)
    def _():
        kbuf[0] = jnp.zeros(kbuf.shape[1:], kbuf.dtype)
        vbuf[0] = jnp.zeros(vbuf.shape[1:], vbuf.dtype)

    @pl.when(r == 0)
    def _():
        kbuf[1] = jnp.zeros(kbuf.shape[1:], kbuf.dtype)
        vbuf[1] = jnp.zeros(vbuf.shape[1:], vbuf.dtype)

    sign = jnp.where(lax.broadcasted_iota(jnp.int32, (1, HD), 1) < HD // 2, -1.0, 1.0)
    key_base = r * tok - 2 * tok

    def table(i, _):
        at = pl.multiple_of(i * 128, 128)
        pos = (key_base + at + lax.broadcasted_iota(jnp.int32, (128, HD), 0)).astype(jnp.float32)
        ang = pos * inv_ref[...]
        cosb[pl.ds(at, 128), :] = jnp.cos(ang)
        sinb[pl.ds(at, 128), :] = jnp.sin(ang) * sign
        return 0

    lax.fori_loop(0, 3 * tok // 128, table, 0)

    def turned(x, at):
        x = x.astype(jnp.float32)
        cs, sn = cosb[pl.ds(at, 128), :], sinb[pl.ds(at, 128), :]
        return (x * cs + pltpu.roll(x, HD // 2, 1) * sn).astype(jnp.bfloat16)

    loc[2].wait()

    def rot_q(i, _):
        at = pl.multiple_of(i * 128, 128)
        for h in range(heads):
            cols = slice(h * HD, (h + 1) * HD)
            qbuf[pl.ds(at, 128), cols] = turned(qbuf[pl.ds(at, 128), cols], 2 * tok + at)
        return 0

    lax.fori_loop(0, tok // 128, rot_q, 0)

    def rot_k(slot):
        def body(i, _):
            at = pl.multiple_of(i * 128, 128)
            for h in range(kvh):
                cols = slice(h * HD, (h + 1) * HD)
                krot[pl.ds(slot * tok + at, 128), cols] = turned(kbuf[slot, pl.ds(at, 128), cols], slot * tok + at)
            return 0

        lax.fori_loop(0, tok // 128, body, 0)

    loc[1].wait()
    loc[3].wait()
    rot_k(2)

    def prep(i, _):
        at = pl.multiple_of(i * TN, 128)
        ein_cat[pl.ds(at, TN), :] = split_cat(ein_ref[pl.ds(at, TN), :])
        eout_cat[pl.ds(at, TN), :] = split_cat(eout_ref[pl.ds(at, TN), :])
        return 0

    lax.fori_loop(0, n_tile, prep, 0)

    m_hi, m_lo = hi_lo(jnp.broadcast_to(mean_ref[...], (16, half)))
    m_acc = jnp.dot(m_hi, ein_cat[...], preferred_element_type=jnp.float32) + jnp.dot(
        m_lo, ein_cat[...], preferred_element_type=jnp.float32)
    st_send[tok:tok + 8, :] = (m_acc + pltpu.roll(m_acc, HD // 2, 1))[0:8]

    def z_event(k):
        below, above = zz - k >= 0, zz + k < nz
        for cond, src_z, onward, can in ((below, zz - k, up, has_up), (above, zz + k, dn, has_dn)):
            u = unit(g, src_z, yy)

            @pl.when(cond)
            def _():
                wait_w(u)

            send_w(cond & can, u, onward)
            send_w(cond, u, ynb)
            send_w(cond, u, xnb)

    def d_event(k):
        for cond, src_z in ((zz - k >= 0, zz - k), (zz + k < nz, zz + k)):
            u = unit(g, src_z, 1 - yy)

            @pl.when(cond)
            def _():
                wait_w(u)

            send_w(cond, u, xnb)

    z_event(1)

    @pl.when(zz > 0)
    def _():
        wait_kv(0)

    relay = (zz > 0) & (yy == 1)
    send_kv(relay, lambda: kbuf.at[0], kbuf, 1, 0, ynb)
    send_kv(relay, lambda: vbuf.at[0], vbuf, 1, 1, ynb)
    rot_k(0)
    d_event(1)
    z_event(2)
    send_w(None, u_other, ynb)

    @pl.when(r > 0)
    def _():
        wait_kv(1)

    rot_k(1)

    nt = WINDOW // QB + 1
    ri = lax.broadcasted_iota(jnp.int32, (QB, QB), 0)
    ci = lax.broadcasted_iota(jnp.int32, (QB, QB), 1)
    per = tok // QB
    pen = [jnp.where(zz > 0, 0.0, BIG), jnp.where(r > 0, 0.0, BIG), jnp.float32(0.0)]

    def make_att(p):
        cols = pl.ds(pl.multiple_of(f * acols + p * 2 * HD, 128), 2 * HD)
        return pltpu.make_async_remote_copy(
            src_ref=att.at[:, cols], dst_ref=att.at[:, cols], send_sem=as_sem.at[p], recv_sem=ar_sem.at[p],
            device_id=part, device_id_type=MESH)

    def wait_att(p):
        cols = pl.ds(pl.multiple_of((1 - f) * acols + p * 2 * HD, 128), 2 * HD)
        pltpu.make_async_copy(att.at[:, cols], att.at[:, cols], ar_sem.at[p]).wait()

    def piece(j, _):
        head, i = j // per, j % per
        kv = head // (heads // kvh)
        qt = qbuf[pl.ds(pl.multiple_of(i * QB, QB), QB), pl.ds(pl.multiple_of(head * HD, HD), HD)]
        key_rows = pl.ds(pl.multiple_of(i * QB, QB), nt * QB)
        kv_cols = pl.ds(pl.multiple_of(kv * HD, HD), HD)
        s = lax.dot_general(qt, krot[key_rows, kv_cols], (((1,), (1,)), ((), ())),
                            preferred_element_type=jnp.float32) * query_scale
        tiles, bias, m = [], [], None
        for t in range(nt):
            st = s[:, t * QB:(t + 1) * QB]
            if t == 0:
                st = jnp.where(ci > ri, st, -BIG)
            if t == nt - 1:
                st = jnp.where(ci <= ri, st, -BIG)
            blk = (i + t) // per
            b = jnp.where(blk == 0, pen[0], jnp.where(blk == 1, pen[1], pen[2]))
            mt = jnp.max(st, axis=1, keepdims=True) - b
            m = mt if m is None else jnp.maximum(m, mt)
            tiles.append(st)
            bias.append(b)
        es, tot = [], None
        for st, b in zip(tiles, bias):
            e = jnp.exp(st - (m + b))
            es.append(e)
            se = jnp.sum(e, axis=1, keepdims=True)
            tot = se if tot is None else tot + se
        inv = 1.0 / tot
        p = jnp.concatenate([(e * inv).astype(jnp.bfloat16) for e in es], axis=1)
        o = jnp.dot(p, vflat[key_rows, kv_cols], preferred_element_type=jnp.float32)
        att[pl.ds(pl.multiple_of(i * QB, QB), QB),
            pl.ds(pl.multiple_of(f * acols + head * HD, HD), HD)] = o.astype(jnp.bfloat16)

        for pp in range(heads // 2 - 1):
            @pl.when(j == (2 * pp + 3) * per)
            def _():
                make_att(pp).start()
        return 0

    vflat = vbuf.reshape(3 * tok, kvh * HD)
    n_piece = heads * per
    if nz == 4:
        lax.fori_loop(0, n_piece // 2, piece, 0)
        z_event(3)
        d_event(2)
        lax.fori_loop(n_piece // 2, n_piece, piece, 0)
    else:
        lax.fori_loop(0, n_piece, piece, 0)
    make_att(heads // 2 - 1).start()
    if nz == 4:
        d_event(3)
    else:
        for k in range(3, nz):
            z_event(k)
        for k in range(2, nz):
            d_event(k)

    def mm(first, chunks):
        def body(n, _):
            cols = pl.ds(pl.multiple_of(n * TN, 128), TN)
            acc = None if first else hidden[:, cols]
            for w_at, a_at in chunks:
                cnt = QB // rows
                wt = wbuf[pl.ds(w_at, cnt), :, cols].reshape(QB, TN)
                d = jnp.dot(att[:, pl.ds(pl.multiple_of(a_at, 128), QB)], wt, preferred_element_type=jnp.float32)
                acc = d if acc is None else acc + d
            hidden[:, cols] = acc
            return 0

        lax.fori_loop(0, n_tile, body, 0)

    wait_w(unit(0, zz, 1 - yy))
    wait_w(unit(1, zz, 1 - yy))
    for p in range(heads // 2):
        make_att(p).wait_send()
        wait_att(p)
    if rows == HD:
        def plane(first, z):
            mm(first, [(unit(c, z, 0), unit(c, z, 0) * rows) for c in range(2)])

        plane(True, zz)
        for k in range(1, nz):
            for cond, src_z in ((zz - k >= 0, zz - k), (zz + k < nz, zz + k)):
                @pl.when(cond)
                def _():
                    wait_w(unit(1 - g, src_z, yy))
                    wait_w(unit(1 - g, src_z, 1 - yy))
                    plane(False, src_z)
    else:
        for k in range(1, nz):
            for cond, src_z in ((zz - k >= 0, zz - k), (zz + k < nz, zz + k)):
                @pl.when(cond)
                def _():
                    wait_w(unit(1 - g, src_z, yy))
                    wait_w(unit(1 - g, src_z, 1 - yy))
        cnt = QB // rows
        for c in range(wbuf.shape[0] // cnt):
            mm(c == 0, [(c * cnt, c * QB)])

    lane = lax.broadcasted_iota(jnp.int32, (tok, HD), 1)

    def stats(n, carry):
        code, sq = carry
        cols = pl.ds(pl.multiple_of(n * TN, 128), TN)
        h = hidden[:, cols]
        sq = sq + jnp.sum(h * h, axis=1, keepdims=True)
        hi, lo = hi_lo(h * gain_ref[:, cols])
        e = ein_cat[cols, :]
        code = code + jnp.dot(hi, e, preferred_element_type=jnp.float32) + jnp.dot(
            lo, e, preferred_element_type=jnp.float32)
        return code, sq

    code, sq = lax.fori_loop(0, n_tile, stats, (jnp.zeros((tok, HD), jnp.float32), jnp.zeros((tok, 1), jnp.float32)))
    code = code + pltpu.roll(code, HD // 2, 1)
    st_send[0:tok, :] = jnp.where(lane < HD // 2, code, sq)
    swap = pltpu.make_async_remote_copy(src_ref=st_send, dst_ref=st_recv, send_sem=ss_sem, recv_sem=sr_sem,
                                        device_id=part, device_id_type=MESH)
    swap.start()
    for cond, make in pending:
        if cond is None:
            make().wait_send()
        else:
            @pl.when(cond)
            def _():
                make().wait_send()
    swap.wait()
    both = st_send[0:tok, :] + st_recv[0:tok, :]
    turned_both = pltpu.roll(both, HD // 2, 1)
    code = jnp.where(lane < HD // 2, both, turned_both)
    total = jnp.where(lane < HD // 2, turned_both, both)
    inv_rms = lax.rsqrt(total * (1.0 / d_full) + norm_eps)
    mean_sum = st_send[tok:tok + 1, :] + st_recv[tok:tok + 1, :]
    c_hi, c_lo = hi_lo(inv_rms * code - mean_sum)
    scale = inv_rms[:, 0:1]

    def finish(n, _):
        cols = pl.ds(pl.multiple_of(n * TN, 128), TN)
        e = eout_cat[cols, :]
        nt_dims = (((1,), (1,)), ((), ()))
        back = lax.dot_general(c_hi, e, nt_dims, preferred_element_type=jnp.float32) + lax.dot_general(
            c_lo, e, nt_dims, preferred_element_type=jnp.float32)
        out_ref[:, cols] = (hidden[:, cols] * scale * gain_ref[:, cols] - back).astype(jnp.bfloat16)
        return 0

    lax.fori_loop(0, n_tile, finish, 0)


def solution(mesh):
    n_row = mesh.shape["row"]

    def on_device(queries, keys, values, out_proj, post_gain, mean_vec, erase_in, erase_out):
        tok = queries.shape[0]
        rows, d_full = out_proj.shape
        half = post_gain.shape[0]
        n_unit = 2 * n_row
        nz = n_row // 2
        half_dim = HD // 2
        inverse = np.exp(-(2.0 * np.arange(half_dim, dtype=np.float32) / HD) * np.log(np.float32(rope_base)))
        inverse = np.concatenate([inverse, inverse]).astype(np.float32)[None, :]
        any_spec = pl.BlockSpec(memory_space=pl.ANY)
        vm = pl.BlockSpec(memory_space=pltpu.VMEM)
        n_ws = 5 + 8 * (nz - 1) + 4
        bf, f32 = jnp.bfloat16, jnp.float32
        dma = pltpu.SemaphoreType.DMA
        return pl.pallas_call(
            functools.partial(kernel, n_row, d_full),
            out_shape=jax.ShapeDtypeStruct((tok, half), bf),
            in_specs=[any_spec] * 4 + [vm] * 5,
            out_specs=vm,
            scratch_shapes=[
                pltpu.VMEM(queries.shape, bf),
                pltpu.VMEM((3,) + keys.shape, bf),
                pltpu.VMEM((3,) + keys.shape, bf),
                pltpu.VMEM((3 * tok, keys.shape[1]), bf),
                pltpu.VMEM((n_unit, rows, half), bf),
                pltpu.VMEM((tok, 2 * queries.shape[1]), bf),
                pltpu.VMEM((tok, half), f32),
                pltpu.VMEM((3 * tok, HD), f32),
                pltpu.VMEM((3 * tok, HD), f32),
                pltpu.VMEM((half, HD), bf),
                pltpu.VMEM((half, HD), bf),
                pltpu.VMEM((tok + 8, HD), f32),
                pltpu.VMEM((tok + 8, HD), f32),
                dma((4,)), dma((n_unit,)), dma((n_ws,)), dma((4,)), dma((6,)),
                dma((4,)), dma((4,)), dma, dma,
            ],
            compiler_params=pltpu.CompilerParams(
                collective_id=0, has_side_effects=True, vmem_limit_bytes=60 * 1024 * 1024),
        )(queries, keys, values, out_proj, post_gain.reshape(1, -1), mean_vec.reshape(1, -1),
          erase_in, erase_out, jnp.asarray(inverse))

    placed = (
        P(("grp", "row"), "col"),
        P(("grp", "row"), "col"),
        P(("grp", "row"), "col"),
        P(("col", "row"), None),
        P("col"),
        P("col"),
        P("col", None),
        P("col", None),
    )
    return jax.shard_map(
        on_device, mesh=mesh, in_specs=placed, out_specs=P(("grp", "row"), "col"), check_vma=False
    )
```

time: 279 us -> 155 us (0.56)
  waiting for transfers between devices: 154 us -> 0 us
  Pallas kernels: 0 us -> 145 us
  matrix products: 64.3 us -> 0 us
  between operations: 13.3 us -> 0.01 us
  starting transfers between devices: 13 us -> 0 us
  other arithmetic: 12.6 us -> 0 us
  local copies, waits for them, and re-layouts: 17.3 us -> 10.3 us
    pallas_call x0 -> x1, Pallas kernels: none -> 145 us  [on_device(): pl.pallas_call(functools.partial(kernel, n_row, d_full), out_shape=jax.Sh...]
    all_gather x1 -> x0, waiting for transfers between devices: 64.3 us -> none  [on_device(): lax.all_gather(out_proj, 'row', axis=0, tiled=True)]
    ppermute x4 -> x0, waiting for transfers between devices: 57.8 us -> none  [shifted(): return lax.ppermute(block, axis, route)]
    dot_general x8 -> x0, matrix products: 34.4 us -> none  [the longest x1 12.6 us: on_device(): jnp.dot(attended, lax.all_gather(out_proj, 'row', axis=0, tiled=True), pr...]
    sub x4 -> x0, matrix products: 29.9 us -> none  [on_device(): weights = jnp.where(allowed, jnp.exp(scores - row_max), 0.0)]
    reduce_scatter x1 -> x0, waiting for transfers between devices: 17.2 us -> none  [on_device(): lax.psum_scatter(partial_sum, 'col', scatter_dimension=1, tiled=True)]
    psum x1 -> x0, waiting for transfers between devices: 14.2 us -> none  [on_device(): lax.psum((jnp.sum(hidden * hidden, axis=1), gained, mean_code), 'col')]
    ppermute x4 -> x0, starting transfers between devices: 12.7 us -> none  [shifted(): return lax.ppermute(block, axis, route)]
  transfers between devices with their start and end apart: 7 -> 0, of which waited for: 6 -> 0; matrix products, arithmetic and copies ran while one was open for 22% -> 0% of each run, Pallas kernels for 0% -> 0%
where the time goes in v1:
time: 155 us
  Pallas kernels  145 us (94%)
  local copies, waits for them, and re-layouts  10.3 us (7%)
    pallas_call x1, Pallas kernels, on_device(): pl.pallas_call(functools.partial(kernel, n_row, d_full), out_shape=jax.Sh...  145 us
    unnamed x5, local copies, waits for them, and re-layouts  7.64 us

profile of v1, /device:TPU:5, one launch (start us, length us, event | category | flops | bytes accessed | tf_op | source)
XLA Modules:
  0.0 155.0 jit_solution(15224310882036266588)
XLA Ops:
  0.0 0.0 copy-start
  0.0 1.4 reshape.6.gain_ref
  1.4 1.3 reshape.7.mean_ref
  2.7 2.6 %copy.10.ein_ref = f32[2688,64]{1,0:T(8,128)} copy(f32[2688,64]{0,1:T(8,128)} %param.15) | data formatting | bytes 1376256 | tf_op args[6]
  5.3 0.0 copy-done
  5.3 1.5 copy.11.eout_ref
  6.8 144.6 %shard_map.91 = bf16[512,2688]{1,0:T(8,128)(2,1)} custom-call(bf16[512,1024]{1,0:T(8,128)(2,1)} %q_hbm.1, bf16[512,512]{1,0:T(8,128)(2,1)} %k_hbm.1, bf16[512,512]{1,0:T(8,128)(2,1)} %v_hbm.1, bf16[128,5376]{1,0:T(8,128)(2,1)} %w_hbm.1, f32[1,2688]{1,0:T(1,128)} %reshape.6.gain_ref, f32[1,2688]{1,0:T(1,128)} %reshape.7.mean_ref, f32[2688,64]{1,0:T(8,128)} %copy.10.ein_ref, ...), custom_call_target="tpu_custom_call" | custom-call | tf_op jit(solution)/shard_map/pallas_call | solution.py:426
  151.5 3.5 %copy.13 = bf16[512,2688]{1,0:T(8,128)(2,1)} copy(bf16[512,2688]{1,0:T(8,128)(2,1)} %shard_map.91) | data formatting | bytes 5505024
Async XLA Ops:
  0.0 5.3 %copy-start = (f32[2688,64]{0,1:T(8,128)S(1)}, f32[2688,64]{0,1:T(8,128)}, u32[]{:S(2)}) copy-start(f32[2688,64]{0,1:T(8,128)} %param.16) | copy-start | bytes 2064388

commit v2 on v1

--- a/solution.py
+++ b/solution.py
@@ -21,7 +21,7 @@
 
 def split_cat(x):
     hi = x.astype(jnp.bfloat16).astype(jnp.float32)
-    return jnp.concatenate([hi, x - hi], axis=1).astype(jnp.bfloat16)
+    return jnp.concatenate([hi, x - hi], axis=0).astype(jnp.bfloat16)
 
 
 def hi_lo(x):
@@ -29,7 +29,11 @@
     return hi, (x - hi.astype(jnp.float32)).astype(jnp.bfloat16)
 
 
-def kernel(n_row, d_full, q_hbm, k_hbm, v_hbm, w_hbm, gain_ref, mean_ref, ein_ref, eout_ref, inv_ref,
+def dot_nt(x, y):
+    return lax.dot_general(x, y, (((1,), (1,)), ((), ())), preferred_element_type=jnp.float32)
+
+
+def kernel(n_row, d_full, parts, q_hbm, k_hbm, v_hbm, w_hbm, gain_ref, mean_ref, ein_ref, eout_ref, inv_ref,
            out_ref, qbuf, kbuf, vbuf, krot, wbuf, att, hidden, cosb, sinb, ein_cat, eout_cat,
            st_send, st_recv, loc_sem, wr_sem, ws_sem, kr_sem, ks_sem, as_sem, ar_sem, ss_sem, sr_sem):
     nz = n_row // 2
@@ -37,7 +41,8 @@
     zz, yy = r // 2, r % 2
     has_up, has_dn = zz < nz - 1, zz > 0
     tok = qbuf.shape[0]
-    rows, half = wbuf.shape[1], wbuf.shape[2]
+    sub, half = wbuf.shape[1], wbuf.shape[2]
+    rows = sub * parts
     heads = qbuf.shape[1] // HD
     kvh = kbuf.shape[2] // HD
     acols = heads * HD
@@ -62,11 +67,15 @@
         pl.semaphore_signal(barrier, inc=1, device_id=dn, device_id_type=MESH)
 
     u_own = f * n_row + r
-    loc = [
-        pltpu.make_async_copy(w_hbm.at[:, pl.ds(pl.multiple_of(f * half, 128), half)], wbuf.at[u_own], loc_sem.at[0]),
-        pltpu.make_async_copy(k_hbm, kbuf.at[2], loc_sem.at[1]),
-        pltpu.make_async_copy(q_hbm, qbuf, loc_sem.at[2]),
-        pltpu.make_async_copy(v_hbm, vbuf.at[2], loc_sem.at[3]),
+
+    def own_w(s, c):
+        return w_hbm.at[pl.ds(s * sub, sub), pl.ds(pl.multiple_of(c * half, 128), half)]
+
+    loc_w = [pltpu.make_async_copy(own_w(s, f), wbuf.at[u_own * parts + s], loc_sem.at[3 + s]) for s in range(parts)]
+    loc = loc_w + [
+        pltpu.make_async_copy(k_hbm, kbuf.at[2], loc_sem.at[0]),
+        pltpu.make_async_copy(q_hbm, qbuf, loc_sem.at[1]),
+        pltpu.make_async_copy(v_hbm, vbuf.at[2], loc_sem.at[2]),
     ]
     for c in loc:
         c.start()
@@ -86,14 +95,15 @@
 
     n_ws = [0]
 
-    def send_w(cond, u, dev, src=None):
+    def send_w(cond, u, s, dev, src=None):
         i = n_ws[0]
         n_ws[0] += 1
 
         def make():
+            slot = u * parts + s
             return pltpu.make_async_remote_copy(
-                src_ref=wbuf.at[u] if src is None else src(), dst_ref=wbuf.at[u],
-                send_sem=ws_sem.at[i], recv_sem=wr_sem.at[u], device_id=dev, device_id_type=MESH)
+                src_ref=wbuf.at[slot] if src is None else src(), dst_ref=wbuf.at[slot],
+                send_sem=ws_sem.at[i], recv_sem=wr_sem.at[slot], device_id=dev, device_id_type=MESH)
 
         send(cond, make)
 
@@ -110,29 +120,31 @@
 
         send(cond, make)
 
-    def wait_w(u):
-        pltpu.make_async_copy(wbuf.at[u], wbuf.at[u], wr_sem.at[u]).wait()
+    def wait_w(u, s):
+        slot = u * parts + s
+        pltpu.make_async_copy(wbuf.at[slot], wbuf.at[slot], wr_sem.at[slot]).wait()
+
+    every = range(parts)
 
     def wait_kv(slot):
         pltpu.make_async_copy(kbuf.at[slot], kbuf.at[slot], kr_sem.at[2 * slot]).wait()
         pltpu.make_async_copy(vbuf.at[slot], vbuf.at[slot], kr_sem.at[2 * slot + 1]).wait()
 
-    send_w(None, u_own, part, lambda: w_hbm.at[:, pl.ds(pl.multiple_of((1 - f) * half, 128), half)])
-    send_kv(yy == 0, lambda: k_hbm, kbuf, 1, 0, ynb)
-    send_kv(yy == 0, lambda: v_hbm, vbuf, 1, 1, ynb)
-    send_kv(has_up, lambda: k_hbm, kbuf, 0, 0, up)
+    for s in every:
+        send_w(None, u_own, s, part, lambda s=s: own_w(s, 1 - f))
 
     def unit(c, z, y):
         return c * n_row + 2 * z + y
 
     u_line = unit(g, zz, yy)
-    u_other = unit(1 - g, zz, yy)
-    loc[0].wait()
-    wait_w(unit(1 - f, zz, yy))
-    send_w(has_up, u_line, up)
-    send_w(has_dn, u_line, dn)
+    for s in every:
+        loc_w[s].wait()
+        wait_w(unit(1 - f, zz, yy), s)
+        send_w(has_up, u_line, s, up)
+        send_w(has_dn, u_line, s, dn)
+        send_w(None, u_line, s, ynb)
+    send_kv(has_up, lambda: k_hbm, kbuf, 0, 0, up)
     send_kv(has_up, lambda: v_hbm, vbuf, 0, 1, up)
-    send_w(None, u_line, ynb)
 
     @pl.when(zz == 0)
     def _():
@@ -162,7 +174,7 @@
         cs, sn = cosb[pl.ds(at, 128), :], sinb[pl.ds(at, 128), :]
         return (x * cs + pltpu.roll(x, HD // 2, 1) * sn).astype(jnp.bfloat16)
 
-    loc[2].wait()
+    loc[parts + 1].wait()
 
     def rot_q(i, _):
         at = pl.multiple_of(i * 128, 128)
@@ -183,47 +195,65 @@
 
         lax.fori_loop(0, tok // 128, body, 0)
 
-    loc[1].wait()
-    loc[3].wait()
+    loc[parts].wait()
+    loc[parts + 2].wait()
     rot_k(2)
 
     def prep(i, _):
         at = pl.multiple_of(i * TN, 128)
-        ein_cat[pl.ds(at, TN), :] = split_cat(ein_ref[pl.ds(at, TN), :])
-        eout_cat[pl.ds(at, TN), :] = split_cat(eout_ref[pl.ds(at, TN), :])
+        ein_cat[:, pl.ds(at, TN)] = split_cat(ein_ref[:, pl.ds(at, TN)])
+        eout_cat[:, pl.ds(at, TN)] = split_cat(eout_ref[:, pl.ds(at, TN)])
         return 0
 
     lax.fori_loop(0, n_tile, prep, 0)
 
-    m_hi, m_lo = hi_lo(jnp.broadcast_to(mean_ref[...], (16, half)))
-    m_acc = jnp.dot(m_hi, ein_cat[...], preferred_element_type=jnp.float32) + jnp.dot(
-        m_lo, ein_cat[...], preferred_element_type=jnp.float32)
+    m_hi, m_lo = hi_lo(jnp.broadcast_to(mean_ref[...][None, :], (16, half)))
+    m_acc = dot_nt(m_hi, ein_cat[...]) + dot_nt(m_lo, ein_cat[...])
     st_send[tok:tok + 8, :] = (m_acc + pltpu.roll(m_acc, HD // 2, 1))[0:8]
 
-    def z_event(k):
-        below, above = zz - k >= 0, zz + k < nz
-        for cond, src_z, onward, can in ((below, zz - k, up, has_up), (above, zz + k, dn, has_dn)):
-            u = unit(g, src_z, yy)
-
+    def side(cond, z, onward, can):
+        return cond, cond & can, z, onward, unit(g, z, yy), unit(g, z, 1 - yy), unit(1 - g, z, yy)
+
+    near = [None] + [
+        (side(zz - k >= 0, zz - k, up, has_up), side(zz + k < nz, zz + k, dn, has_dn)) for k in range(1, nz)
+    ]
+
+    def z_event(k, s):
+        for cond, further, _, onward, u, _, _ in near[k]:
             @pl.when(cond)
             def _():
-                wait_w(u)
-
-            send_w(cond & can, u, onward)
-            send_w(cond, u, ynb)
-            send_w(cond, u, xnb)
-
-    def d_event(k):
-        for cond, src_z in ((zz - k >= 0, zz - k), (zz + k < nz, zz + k)):
-            u = unit(g, src_z, 1 - yy)
+                wait_w(u, s)
+
+            if k < nz - 1:
+                send_w(further, u, s, onward)
+            send_w(cond, u, s, ynb)
+            send_w(cond, u, s, xnb)
+
+    def by_y(k, s):
+        return parts > 1 and s >= parts // 2 and k in (nz - 1, nz - 2)
+
+    def d_event(k, s):
+        for cond, _, _, _, _, u_y, u_x in near[k]:
+            u = u_x if by_y(k, s) else u_y
 
             @pl.when(cond)
             def _():
-                wait_w(u)
-
-            send_w(cond, u, xnb)
-
-    z_event(1)
+                wait_w(u, s)
+
+            send_w(cond, u, s, ynb if by_y(k, s) else xnb)
+
+    def own_to_x(s):
+        u = unit(g, zz, 1 - yy)
+        wait_w(u, s)
+        send_w(None, u, s, xnb)
+
+    for s in every:
+        z_event(1, s)
+        own_to_x(s)
+    send_kv(yy == 0, lambda: k_hbm, kbuf, 1, 0, ynb)
+    send_kv(yy == 0, lambda: v_hbm, vbuf, 1, 1, ynb)
+    for s in every:
+        d_event(1, s)
 
     @pl.when(zz > 0)
     def _():
@@ -233,9 +263,11 @@
     send_kv(relay, lambda: kbuf.at[0], kbuf, 1, 0, ynb)
     send_kv(relay, lambda: vbuf.at[0], vbuf, 1, 1, ynb)
     rot_k(0)
-    d_event(1)
-    z_event(2)
-    send_w(None, u_other, ynb)
+    for s in every:
+        z_event(2, s)
+    if nz == 4:
+        for s in range(parts // 2):
+            z_event(3, s)
 
     @pl.when(r > 0)
     def _():
@@ -265,8 +297,7 @@
         qt = qbuf[pl.ds(pl.multiple_of(i * QB, QB), QB), pl.ds(pl.multiple_of(head * HD, HD), HD)]
         key_rows = pl.ds(pl.multiple_of(i * QB, QB), nt * QB)
         kv_cols = pl.ds(pl.multiple_of(kv * HD, HD), HD)
-        s = lax.dot_general(qt, krot[key_rows, kv_cols], (((1,), (1,)), ((), ())),
-                            preferred_element_type=jnp.float32) * query_scale
+        s = dot_nt(qt, krot[key_rows, kv_cols]) * query_scale
         tiles, bias, m = [], [], None
         for t in range(nt):
             st = s[:, t * QB:(t + 1) * QB]
@@ -301,27 +332,33 @@
     vflat = vbuf.reshape(3 * tok, kvh * HD)
     n_piece = heads * per
     if nz == 4:
-        lax.fori_loop(0, n_piece // 2, piece, 0)
-        z_event(3)
-        d_event(2)
-        lax.fori_loop(n_piece // 2, n_piece, piece, 0)
+        late = [(z_event, 3, s) for s in range(parts // 2, parts)] + [(d_event, k, s) for k in (2, 3) for s in every]
+        inside = late
     else:
-        lax.fori_loop(0, n_piece, piece, 0)
+        late = [(d_event, 2, s) for s in every]
+        for k in range(3, nz):
+            late += [(z_event, k, s) for s in every] + [(d_event, k, s) for s in every]
+        inside = []
+
+    def steps(j, _):
+        piece(j, 0)
+        for n, (event, k, s) in enumerate(inside):
+            @pl.when(j == 1 + (3 * n) // 2)
+            def _():
+                event(k, s)
+        return 0
+
+    lax.fori_loop(0, n_piece, steps, 0)
     make_att(heads // 2 - 1).start()
-    if nz == 4:
-        d_event(3)
-    else:
-        for k in range(3, nz):
-            z_event(k)
-        for k in range(2, nz):
-            d_event(k)
+    for event, k, s in late[len(inside):]:
+        event(k, s)
 
     def mm(first, chunks):
         def body(n, _):
             cols = pl.ds(pl.multiple_of(n * TN, 128), TN)
             acc = None if first else hidden[:, cols]
             for w_at, a_at in chunks:
-                cnt = QB // rows
+                cnt = QB // sub
                 wt = wbuf[pl.ds(w_at, cnt), :, cols].reshape(QB, TN)
                 d = jnp.dot(att[:, pl.ds(pl.multiple_of(a_at, 128), QB)], wt, preferred_element_type=jnp.float32)
                 acc = d if acc is None else acc + d
@@ -330,31 +367,35 @@
 
         lax.fori_loop(0, n_tile, body, 0)
 
-    wait_w(unit(0, zz, 1 - yy))
-    wait_w(unit(1, zz, 1 - yy))
+    for s in every:
+        wait_w(unit(1 - g, zz, 1 - yy), s)
     for p in range(heads // 2):
         make_att(p).wait_send()
         wait_att(p)
+
+    def wait_rest(k, z):
+        for s in every:
+            wait_w(unit(1 - g, z, 1 - yy), s)
+            wait_w(unit(g, z, 1 - yy) if by_y(k, s) else unit(1 - g, z, yy), s)
+
     if rows == HD:
         def plane(first, z):
-            mm(first, [(unit(c, z, 0), unit(c, z, 0) * rows) for c in range(2)])
+            mm(first, [(unit(c, z, 0) * parts, unit(c, z, 0) * rows) for c in range(2)])
 
         plane(True, zz)
         for k in range(1, nz):
-            for cond, src_z in ((zz - k >= 0, zz - k), (zz + k < nz, zz + k)):
+            for cond, _, z, _, _, _, _ in near[k]:
                 @pl.when(cond)
                 def _():
-                    wait_w(unit(1 - g, src_z, yy))
-                    wait_w(unit(1 - g, src_z, 1 - yy))
-                    plane(False, src_z)
+                    wait_rest(k, z)
+                    plane(False, z)
     else:
         for k in range(1, nz):
-            for cond, src_z in ((zz - k >= 0, zz - k), (zz + k < nz, zz + k)):
+            for cond, _, z, _, _, _, _ in near[k]:
                 @pl.when(cond)
                 def _():
-                    wait_w(unit(1 - g, src_z, yy))
-                    wait_w(unit(1 - g, src_z, 1 - yy))
-        cnt = QB // rows
+                    wait_rest(k, z)
+        cnt = QB // sub
         for c in range(wbuf.shape[0] // cnt):
             mm(c == 0, [(c * cnt, c * QB)])
 
@@ -365,10 +406,9 @@
         cols = pl.ds(pl.multiple_of(n * TN, 128), TN)
         h = hidden[:, cols]
         sq = sq + jnp.sum(h * h, axis=1, keepdims=True)
-        hi, lo = hi_lo(h * gain_ref[:, cols])
-        e = ein_cat[cols, :]
-        code = code + jnp.dot(hi, e, preferred_element_type=jnp.float32) + jnp.dot(
-            lo, e, preferred_element_type=jnp.float32)
+        hi, lo = hi_lo(h * gain_ref[cols][None, :])
+        e = ein_cat[:, cols]
+        code = code + dot_nt(hi, e) + dot_nt(lo, e)
         return code, sq
 
     code, sq = lax.fori_loop(0, n_tile, stats, (jnp.zeros((tok, HD), jnp.float32), jnp.zeros((tok, 1), jnp.float32)))
@@ -396,11 +436,10 @@
 
     def finish(n, _):
         cols = pl.ds(pl.multiple_of(n * TN, 128), TN)
-        e = eout_cat[cols, :]
-        nt_dims = (((1,), (1,)), ((), ()))
-        back = lax.dot_general(c_hi, e, nt_dims, preferred_element_type=jnp.float32) + lax.dot_general(
-            c_lo, e, nt_dims, preferred_element_type=jnp.float32)
-        out_ref[:, cols] = (hidden[:, cols] * scale * gain_ref[:, cols] - back).astype(jnp.bfloat16)
+        e = eout_cat[:, cols]
+        back = jnp.dot(c_hi, e, preferred_element_type=jnp.float32) + jnp.dot(
+            c_lo, e, preferred_element_type=jnp.float32)
+        out_ref[:, cols] = (hidden[:, cols] * scale * gain_ref[cols][None, :] - back).astype(jnp.bfloat16)
         return 0
 
     lax.fori_loop(0, n_tile, finish, 0)
@@ -420,11 +459,12 @@
         inverse = np.concatenate([inverse, inverse]).astype(np.float32)[None, :]
         any_spec = pl.BlockSpec(memory_space=pl.ANY)
         vm = pl.BlockSpec(memory_space=pltpu.VMEM)
-        n_ws = 5 + 8 * (nz - 1) + 4
+        parts = 4 if rows >= 64 else 1
+        n_ws = parts * (8 + 8 * nz)
         bf, f32 = jnp.bfloat16, jnp.float32
         dma = pltpu.SemaphoreType.DMA
         return pl.pallas_call(
-            functools.partial(kernel, n_row, d_full),
+            functools.partial(kernel, n_row, d_full, parts),
             out_shape=jax.ShapeDtypeStruct((tok, half), bf),
             in_specs=[any_spec] * 4 + [vm] * 5,
             out_specs=vm,
@@ -433,22 +473,22 @@
                 pltpu.VMEM((3,) + keys.shape, bf),
                 pltpu.VMEM((3,) + keys.shape, bf),
                 pltpu.VMEM((3 * tok, keys.shape[1]), bf),
-                pltpu.VMEM((n_unit, rows, half), bf),
+                pltpu.VMEM((n_unit * parts, rows // parts, half), bf),
                 pltpu.VMEM((tok, 2 * queries.shape[1]), bf),
                 pltpu.VMEM((tok, half), f32),
                 pltpu.VMEM((3 * tok, HD), f32),
                 pltpu.VMEM((3 * tok, HD), f32),
-                pltpu.VMEM((half, HD), bf),
-                pltpu.VMEM((half, HD), bf),
+                pltpu.VMEM((HD, half), bf),
+                pltpu.VMEM((HD, half), bf),
                 pltpu.VMEM((tok + 8, HD), f32),
                 pltpu.VMEM((tok + 8, HD), f32),
-                dma((4,)), dma((n_unit,)), dma((n_ws,)), dma((4,)), dma((6,)),
+                dma((3 + parts,)), dma((n_unit * parts,)), dma((n_ws,)), dma((4,)), dma((6,)),
                 dma((4,)), dma((4,)), dma, dma,
             ],
             compiler_params=pltpu.CompilerParams(
                 collective_id=0, has_side_effects=True, vmem_limit_bytes=60 * 1024 * 1024),
-        )(queries, keys, values, out_proj, post_gain.reshape(1, -1), mean_vec.reshape(1, -1),
-          erase_in, erase_out, jnp.asarray(inverse))
+        )(queries, keys, values, out_proj, post_gain, mean_vec,
+          erase_in.T, erase_out.T, jnp.asarray(inverse))
 
     placed = (
         P(("grp", "row"), "col"),

time: 155 us -> 139 us (0.90)
  the two profiles are of different devices: /device:TPU:5 before, /device:TPU:21 now
where the time goes in v2:
time: 139 us
  Pallas kernels  135 us (97%)
  local copies, waits for them, and re-layouts  3.5 us (3%)
    pallas_call x1, Pallas kernels, on_device(): pl.pallas_call(functools.partial(kernel, n_row, d_full, parts), out_shape...  135 us
    unnamed x1, local copies, waits for them, and re-layouts  3.5 us

profile of v2, /device:TPU:21, one launch (start us, length us, event | category | flops | bytes accessed | tf_op | source)
XLA Modules:
  0.0 138.8 jit_solution(12070220010911278373)
XLA Ops:
  0.0 135.3 %shard_map.91 = bf16[512,2688]{1,0:T(8,128)(2,1)} custom-call(bf16[512,1024]{1,0:T(8,128)(2,1)} %q_hbm.1, bf16[512,512]{1,0:T(8,128)(2,1)} %k_hbm.1, bf16[512,512]{1,0:T(8,128)(2,1)} %v_hbm.1, bf16[128,5376]{1,0:T(8,128)(2,1)} %w_hbm.1, f32[2688]{0:T(1024)} %gain_ref.1, f32[2688]{0:T(1024)} %mean_ref.1, f32[64,2688]{1,0:T(8,128)} %bitcast.2, ...), custom_call_target="tpu_custom_call" | custom-call | tf_op jit(solution)/shard_map/pallas_call | solution.py:466
  135.3 3.5 %copy.11 = bf16[512,2688]{1,0:T(8,128)(2,1)} copy(bf16[512,2688]{1,0:T(8,128)(2,1)} %shard_map.91) | data formatting | bytes 5505024
